TPU v7x, 32 devices: a whole 2x2x4 slice. The times are simulated.
32 devices in a mesh: grp: 2 (over y), tile: 4 (over z), tm: 2 (over x), ch: 2 (over core).
Axes of the slice: x: 2, y: 2, z: 4, core: 2. Of those that a mesh axis runs over, the one named last changes fastest.
Arguments:
- latent: bfloat16 [8, 8, 64, 512], P(('grp', 'tm'), None, 'tile', 'ch'), parts along dimension 0, may hold values from -340 to 340
- norm_gain: float32 [512], P('ch'), may hold values from 0.1 to 1.9
- norm_shift: float32 [512], P('ch'), may hold values from -3 to 3
- kernel: bfloat16 [3, 3, 3, 512, 512], P(None, None, None, ('ch', 'tile', 'tm')), may hold values from -0.0546875 to 0.0546875
- conv_bias: float32 [512], P('ch'), may hold values from -3 to 3
- blend_profile: int32 [4], replicated, may hold values from 0 to 3
Outputs:
- decoded: bfloat16 [8, 8, 64, 512], P(('grp', 'tm'), None, 'tile', 'ch'), parts along dimension 0
There are 2 independent parts, one for each index of `grp`. A program takes and returns all parts, laid end to end along the dimension named above; an argument that names none is the same for every part. Nothing has to cross between parts.
All inputs are finite; a program needn't handle non-finite values.
Results may differ from a plain program's by a relative error of at most 0.0038.
The roundings to bfloat16 on the way count: a program that leaves them out, or rounds other values in their place, can miss the bound.
Values may be sent and summed in bfloat16 or wider, within the bound.
A program may use at most 64 MiB of HBM per device.

v0:
```python
import jax
import jax.numpy as jnp
from jax import lax
from jax.sharding import PartitionSpec as P

GROUPS = 32
RIM = 4


def with_halo(shard, sides, width):
    for axis, dim in sides:
        size, length = (lax.axis_size(axis), shard.shape[dim])
        up = [(i, (i + 1) % size) for i in range(size - 1)]
        down = [(j, i) for i, j in up]
        last = lax.slice_in_dim(shard, length - width, length, axis=dim)
        leading = lax.slice_in_dim(shard, 0, width, axis=dim)
        before = lax.ppermute(last, axis, up)
        after = lax.ppermute(leading, axis, down)
        shard = jnp.concatenate([before, shard, after], axis=dim)
    return shard


def passed_along(block, axis, distance):
    devices = range(lax.axis_size(axis))
    route = [(i - distance, i) for i in devices if i - distance in devices]
    return lax.ppermute(block, axis, route)


def ramp_weight(profile, position, margin):
    fraction = (position.astype(jnp.float32) + 0.5) / (2.0 * margin)
    exponent = 1.0 + profile.astype(jnp.float32)
    near_part = jnp.power(1.0 - fraction, exponent)
    far_part = jnp.power(fraction, exponent)
    return near_part / (near_part + far_part)


def frame_stats(values, colmask, groups):
    frame_count, row_count, col_count, chan_count = values.shape
    grouped = values.reshape(frame_count, row_count, col_count, groups, chan_count // groups)
    weight = colmask.reshape(1, 1, col_count, 1, 1)
    counted = row_count * (chan_count // groups) * jnp.sum(colmask)
    center = jnp.sum(grouped * weight, axis=(1, 2, 4)) / counted
    spread = (grouped - center[:, None, None, :, None]) * weight
    inverse = lax.rsqrt(jnp.sum(spread * spread, axis=(1, 2, 4)) / counted + 1e-06)
    return (center, inverse)


def activate(values, center, inverse, norm_gain, norm_shift, colmask, timemask, groups):
    frame_count, row_count, col_count, chan_count = values.shape
    grouped = values.reshape(frame_count, row_count, col_count, groups, chan_count // groups)
    normed = (grouped - center[:, None, None, :, None]) * inverse[:, None, None, :, None]
    normed = normed.reshape(values.shape) * norm_gain + norm_shift
    masked = jax.nn.silu(normed) * colmask[None, None, :, None] * timemask[:, None, None, None]
    return masked.astype(jnp.bfloat16)


def conv_taps(padded, kernel_part, frame_count, row_count, col_count):
    in_width = kernel_part.shape[3]
    running = None
    for tap_time in range(3):
        for tap_row in range(3):
            for tap_col in range(3):
                window = padded[
                    tap_time : tap_time + frame_count,
                    tap_row : tap_row + row_count,
                    tap_col : tap_col + col_count,
                ]
                contrib = jnp.dot(
                    window.reshape(-1, in_width),
                    kernel_part[tap_time, tap_row, tap_col],
                    preferred_element_type=jnp.float32,
                )
                running = contrib if running is None else running + contrib
    return running


def on_device(latent, norm_gain, norm_shift, kernel, conv_bias, blend_profile):
    frame_count, row_count, core_cols, chan_half = latent.shape
    out_chans = kernel.shape[4]
    groups = GROUPS // lax.axis_size("ch")
    ncols = core_cols + 2 * RIM
    tile_pos = lax.axis_index("tile")
    tile_count = lax.axis_size("tile")
    window_in = with_halo(latent, (("tile", 2),), RIM)
    cached = passed_along(window_in, "tm", 1)
    frames = jnp.concatenate([cached, window_in], axis=0).astype(jnp.float32)
    column = tile_pos * core_cols - RIM + jnp.arange(ncols, dtype=jnp.int32)
    colmask = ((column >= 0) & (column < tile_count * core_cols)).astype(jnp.float32)
    started = (lax.axis_index("tm") > 0).astype(jnp.float32)
    timemask = jnp.concatenate(
        [jnp.ones((2,), jnp.float32) * started, jnp.ones((frame_count,), jnp.float32)]
    )
    center, inverse = frame_stats(frames, colmask, groups)
    activated = activate(frames, center, inverse, norm_gain, norm_shift, colmask, timemask, groups)
    inputs = (jnp.pad(activated, ((0, 0), (1, 1), (1, 1), (0, 0))),)
    widths = (ncols,)

    def accumulate(shard_rows):
        return tuple(
            (
                conv_taps(source, shard_rows, frame_count, row_count, width_cols)
                for source, width_cols in zip(inputs, widths)
            )
        )

    totals = accumulate(lax.all_gather(kernel, ("tile", "tm"), axis=3, tiled=True))
    shaped = [
        running.reshape(frame_count, row_count, width_cols, out_chans)
        for running, width_cols in zip(totals, widths)
    ]
    joined = shaped[0]
    summed = lax.psum_scatter(joined, "ch", scatter_dimension=3, tiled=True)
    tile_out = (summed + conv_bias).astype(jnp.bfloat16)
    extended = with_halo(tile_out, (("tile", 2),), RIM)
    own_out = tile_out[:, :, RIM : RIM + core_cols]
    left_nbr = extended[:, :, :RIM]
    right_nbr = extended[:, :, ncols + RIM :]
    own_profile = lax.dynamic_index_in_dim(blend_profile, tile_pos, 0, keepdims=False)
    prev_profile = lax.dynamic_index_in_dim(
        blend_profile, jnp.maximum(tile_pos - 1, 0), 0, keepdims=False
    )
    offsets = jnp.arange(RIM, dtype=jnp.int32)
    left_weight = jnp.where(tile_pos > 0, ramp_weight(prev_profile, offsets + RIM, RIM), 0.0)
    right_weight = jnp.where(tile_pos < tile_count - 1, ramp_weight(own_profile, offsets, RIM), 1.0)
    left_wide = left_weight[None, None, :, None]
    right_wide = right_weight[None, None, :, None]
    own_float = own_out.astype(jnp.float32)
    head_cols = own_float[:, :, :RIM] * (1.0 - left_wide) + left_nbr.astype(jnp.float32) * left_wide
    tail_cols = own_float[:, :, core_cols - RIM :] * right_wide + right_nbr.astype(jnp.float32) * (
        1.0 - right_wide
    )
    middle = own_float[:, :, RIM : core_cols - RIM]
    return jnp.concatenate([head_cols, middle, tail_cols], axis=2).astype(jnp.bfloat16)


def solution(mesh):
    in_specs = (
        P(("grp", "tm"), None, "tile", "ch"),
        P("ch"),
        P("ch"),
        P(None, None, None, ("ch", "tile", "tm"), None),
        P("ch"),
        P(),
    )
    out_specs = P(("grp", "tm"), None, "tile", "ch")
    return jax.shard_map(
        on_device, mesh=mesh, in_specs=in_specs, out_specs=out_specs, check_vma=False
    )
```

profile of v0, /device:TPU:0, one launch (start us, length us, event | category | flops | bytes accessed | tf_op | source)
XLA Modules:
  0.0 158.9 jit_solution(7346280072205576620)
XLA Ops:
  6.5 0.7 all-gather.2.cloned.1.call-update
  7.3 0.0 reduce-scatter.2.cloned.1.call-start
  7.3 0.9 fusion.11
  8.2 4.9 %collective-permute-start = (bf16[2,8,4,256]{3,2,1,0:T(4,128)(2,1)S(1)}, bf16[2,8,4,256]{3,2,1,0:T(4,128)(2,1)S(1)}, u32[]{:S(2)}, u32[]{:S(2)}) collective-permute-start(bf16[2,8,4,256]{3,2,1,0:T(4,128)(2,1)S(1)} %get-tuple-element.40), channel_id=1, source_target_pairs={{0,4},{4,8},{8,12},{1,5},{5,9},{9,13},{2,6},{6,10},{10,14},{3,7},{... | collective-permute-start | bytes 98312 | tf_op jit(solution)/shard_map/ppermute | solution.py:17
  13.2 1.3 collective-permute-start.1
  14.5 0.3 collective-permute-done
  14.7 4.2 %collective-permute-done.1 = bf16[2,8,4,256]{3,2,1,0:T(4,128)(2,1)S(1)} collective-permute-done((bf16[2,8,4,256]{3,2,1,0:T(4,128)(2,1)S(1)}, bf16[2,8,4,256]{3,2,1,0:T(4,128)(2,1)S(1)}, u32[]{:S(2)}, u32[]{:S(2)}) %collective-permute-start.1) | collective-permute-done | bytes 32800 | tf_op jit(solution)/shard_map/ppermute | solution.py:18
  19.0 1.0 pad_maximum_fusion.1
  20.0 3.4 %collective-permute-start.2 = (bf16[2,8,24,256]{3,2,1,0:T(8,128)(2,1)S(1)}, bf16[2,8,24,256]{3,2,1,0:T(8,128)(2,1)S(1)}, u32[]{:S(2)}, u32[]{:S(2)}) collective-permute-start(bf16[2,8,24,256]{3,2,1,0:T(8,128)(2,1)S(1)} %pad_maximum_fusion.1), channel_id=1, source_target_pairs={{0,2},{1,3},{4,6},{5,7},{8,10},{9,11},{12,14},{13,15},{16,18},{17,... | collective-permute-start | bytes 589832 | tf_op jit(solution)/shard_map/ppermute | solution.py:26
  23.4 0.6 fusion.9
  24.7 0.5 concatenate.26
  25.2 1.1 concatenate.24
  26.3 5.6 %collective-permute-done.2 = bf16[2,8,24,256]{3,2,1,0:T(8,128)(2,1)S(1)} collective-permute-done((bf16[2,8,24,256]{3,2,1,0:T(8,128)(2,1)S(1)}, bf16[2,8,24,256]{3,2,1,0:T(8,128)(2,1)S(1)}, u32[]{:S(2)}, u32[]{:S(2)}) %collective-permute-start.2) | collective-permute-done | bytes 196640 | tf_op jit(solution)/shard_map/ppermute | solution.py:26
  31.9 1.1 concatenate.23
  32.9 1.2 fusion
  34.2 1.7 %fusion.3 = f32[4,16]{1,0:T(4,128)S(1)} fusion(f32[4,16]{1,0:T(4,128)S(1)} %broadcast_divide_fusion, f32[24]{0:T(128)S(1)} %and_convert_fusion, bf16[2,8,24,16,16]{4,3,2,1,0:T(8,128)(2,1)S(1)} %concatenate.24, bf16[2,8,24,16,16]{4,3,2,1,0:T(8,128)(2,1)S(1)} %concatenate.23), kind=kLoop, calls=%fused_computation.5 | loop fusion | flops 1179584 | bytes 393824 | tf_op jit(solution)/shard_map/reduce_sum | solution.py:44
  35.9 0.1 mul.101
  35.9 0.1 mul.102
  36.0 0.1 sub.64
  36.1 0.1 sub.65
  36.2 0.0 copy-done.1
  36.2 1.1 multiply_convert_fusion
  37.3 1.1 pad_slice_fusion
  38.4 1.3 pad_slice_fusion.1
  39.7 81.3 %all-gather.2.cloned.1.call-done = bf16[3,3,3,256,512]{4,3,2,1,0:T(8,128)(2,1)} async-done(((bf16[3,3,3,32,512]{4,3,2,1,0:T(8,128)(2,1)}), bf16[3,3,3,256,512]{4,3,2,1,0:T(8,128)(2,1)}) %all-gather.2.cloned.1.call-update) | async-done | bytes 7077904 | tf_op jit(solution)/shard_map/all_gather | solution.py:106
  121.1 1.4 fusion.4
  122.5 1.9 %convolution_add_fusion.25 = f32[384,512]{1,0:T(8,128)S(1)} fusion(f32[384,512]{1,0:T(8,128)S(1)} %fusion.4, bf16[384,256]{1,0:T(8,128)(2,1)} %bitcast.161, bf16[3,3,3,256,512]{4,3,2,1,0:T(8,128)(2,1)} %all-gather.2.cloned.1.call-done), kind=kOutput, calls=%fused_computation.56 | convolution fusion | flops 100859904 | bytes 2031616 | tf_op jit(solution)/shard_map/dot_general | solution.py:68
  124.5 1.2 convolution_add_fusion.24
  125.7 1.2 convolution_add_fusion.23
  126.9 0.3 convolution_add_fusion.22
  127.2 0.3 convolution_add_fusion.21
  127.5 0.3 convolution_add_fusion.20
  127.7 0.3 convolution_add_fusion.19
  128.0 0.3 convolution_add_fusion.18
  128.3 0.3 convolution_add_fusion.17
  128.5 0.3 convolution_add_fusion.16
  128.8 0.3 convolution_add_fusion.15
  129.1 0.3 convolution_add_fusion.14
  129.3 0.3 convolution_add_fusion.13
  129.6 0.3 convolution_add_fusion.12
  129.9 0.3 convolution_add_fusion.11
  130.2 0.3 convolution_add_fusion.10
  130.4 0.3 convolution_add_fusion.9
  130.7 0.3 convolution_add_fusion.8
  131.0 0.3 convolution_add_fusion.7
  131.2 0.0 copy-start.9
  131.2 0.0 copy-start.12
  131.3 0.3 convolution_add_fusion.6
  131.5 0.3 convolution_add_fusion.5
  131.8 0.3 convolution_add_fusion.4
  132.1 0.3 convolution_add_fusion.3
  132.4 0.3 convolution_add_fusion.2
  132.6 0.3 convolution_add_fusion.1
  132.9 1.1 convolution_add_fusion
  134.0 0.0 reduce-scatter.2.cloned.1.call-update
  134.1 0.7 fusion.12
  136.1 4.6 %reduce-scatter.2.cloned.1.call-done = f32[2,8,24,256]{3,2,1,0:T(8,128)} async-done(((f32[2,8,24,512]{3,2,1,0:T(8,128)}), f32[2,8,24,256]{3,2,1,0:T(8,128)}) %reduce-scatter.2.cloned.1.call-update) | async-done | bytes 393232 | tf_op jit(solution)/shard_map/reduce_scatter | solution.py:112
  140.7 1.0 add_convert_fusion
  141.7 3.6 %collective-permute-start.3 = (bf16[2,8,4,256]{3,2,1,0:T(4,128)(2,1)S(1)}, bf16[2,8,4,256]{3,2,1,0:T(4,128)(2,1)S(1)}, u32[]{:S(2)}, u32[]{:S(2)}) collective-permute-start(bf16[2,8,4,256]{3,2,1,0:T(4,128)(2,1)S(1)} %get-tuple-element.38), channel_id=1, source_target_pairs={{0,4},{4,8},{8,12},{1,5},{5,9},{9,13},{2,6},{6,10},{10,14},{3,7},{... | collective-permute-start | bytes 98312 | tf_op jit(solution)/shard_map/ppermute | solution.py:17
  145.4 1.3 collective-permute-start.4
  146.7 0.2 collective-permute-done.3
  146.9 4.2 %collective-permute-done.4 = bf16[2,8,4,256]{3,2,1,0:T(4,128)(2,1)S(1)} collective-permute-done((bf16[2,8,4,256]{3,2,1,0:T(4,128)(2,1)S(1)}, bf16[2,8,4,256]{3,2,1,0:T(4,128)(2,1)S(1)}, u32[]{:S(2)}, u32[]{:S(2)}) %collective-permute-start.4) | collective-permute-done | bytes 32800 | tf_op jit(solution)/shard_map/ppermute | solution.py:18
  151.2 0.1 fusion.8
  151.3 0.7 pad_maximum_fusion.2
  (32 shorter events, 0.2 us)
Async XLA Ops:
  6.5 29.7 %copy-start.1 = (bf16[2,8,16,256]{3,2,1,0:T(8,128)(2,1)S(1)}, bf16[2,8,16,256]{3,2,1,0:T(8,128)(2,1)}, u32[]{:S(2)}) copy-start(bf16[2,8,16,256]{3,2,1,0:T(8,128)(2,1)} %param.6) | copy-start | bytes 393220
  6.5 29.7 %copy-start.11 = (f32[256]{0:T(256)S(1)}, f32[256]{0:T(256)}, u32[]{:S(2)}) copy-start(f32[256]{0:T(256)} %param.7) | copy-start | bytes 3076
  6.5 29.7 %copy-start.10 = (f32[256]{0:T(256)S(1)}, f32[256]{0:T(256)}, u32[]{:S(2)}) copy-start(f32[256]{0:T(256)} %param.8) | copy-start | bytes 3076
  6.5 114.5 %all-gather.2.cloned.1.call-start = ((), (), s32[]{:S(2)}) async-start(), calls=%async_computation.1 | async-start | bytes 7962624 | tf_op jit(solution)/shard_map/all_gather | solution.py:106
  7.3 133.4 %reduce-scatter.2.cloned.1.call-start = ((), (), s32[]{:S(2)}) async-start(), calls=%async_computation.2 | async-start | bytes 1179648 | tf_op jit(solution)/shard_map/reduce_scatter | solution.py:112
  8.2 6.5 %collective-permute-start = (bf16[2,8,4,256]{3,2,1,0:T(4,128)(2,1)S(1)}, bf16[2,8,4,256]{3,2,1,0:T(4,128)(2,1)S(1)}, u32[]{:S(2)}, u32[]{:S(2)}) collective-permute-start(bf16[2,8,4,256]{3,2,1,0:T(4,128)(2,1)S(1)} %get-tuple-element.40), channel_id=1, source_target_pairs={{0,4},{4,8},{8,12},{1,5},{5,9},{9,13},{2,6},{6,10},{10,14},{3,7},{... | collective-permute-start | bytes 98312 | tf_op jit(solution)/shard_map/ppermute | solution.py:17
  13.2 5.8 %collective-permute-start.1 = (bf16[2,8,4,256]{3,2,1,0:T(4,128)(2,1)S(1)}, bf16[2,8,4,256]{3,2,1,0:T(4,128)(2,1)S(1)}, u32[]{:S(2)}, u32[]{:S(2)}) collective-permute-start(bf16[2,8,4,256]{3,2,1,0:T(4,128)(2,1)S(1)} %get-tuple-element.41), channel_id=1, source_target_pairs={{4,0},{8,4},{12,8},{5,1},{9,5},{13,9},{6,2},{10,6},{14,10},{7,3},{... | collective-permute-start | bytes 98312 | tf_op jit(solution)/shard_map/ppermute | solution.py:18
  20.0 11.9 %collective-permute-start.2 = (bf16[2,8,24,256]{3,2,1,0:T(8,128)(2,1)S(1)}, bf16[2,8,24,256]{3,2,1,0:T(8,128)(2,1)S(1)}, u32[]{:S(2)}, u32[]{:S(2)}) collective-permute-start(bf16[2,8,24,256]{3,2,1,0:T(8,128)(2,1)S(1)} %pad_maximum_fusion.1), channel_id=1, source_target_pairs={{0,2},{1,3},{4,6},{5,7},{8,10},{9,11},{12,14},{13,15},{16,18},{17,... | collective-permute-start | bytes 589832 | tf_op jit(solution)/shard_map/ppermute | solution.py:26
  121.1 5.8 %copy-start = (bf16[3,3,3,256,512]{4,3,2,1,0:T(8,128)(2,1)S(1)}, bf16[3,3,3,256,512]{4,3,2,1,0:T(8,128)(2,1)}, u32[]{:S(2)}) copy-start(bf16[3,3,3,256,512]{4,3,2,1,0:T(8,128)(2,1)} %all-gather.2.cloned.1.call-done) | copy-start | bytes 21233668
  121.1 5.9 %copy-start.8 = (bf16[2,8,24,256]{3,2,1,0:T(8,128)(2,1)S(1)}, bf16[2,8,24,256]{3,2,1,0:T(8,128)(2,1)}, u32[]{:S(2)}) copy-start(bf16[2,8,24,256]{3,2,1,0:T(8,128)(2,1)} %get-tuple-element.34) | copy-start | bytes 589828
  127.5 1.9 %copy-start.7 = (bf16[2,8,24,256]{3,2,1,0:T(8,128)(2,1)S(1)}, bf16[2,8,24,256]{3,2,1,0:T(8,128)(2,1)}, u32[]{:S(2)}) copy-start(bf16[2,8,24,256]{3,2,1,0:T(8,128)(2,1)} %get-tuple-element.33) | copy-start | bytes 589828
  129.6 1.9 %copy-start.6 = (bf16[2,8,24,256]{3,2,1,0:T(8,128)(2,1)S(1)}, bf16[2,8,24,256]{3,2,1,0:T(8,128)(2,1)}, u32[]{:S(2)}) copy-start(bf16[2,8,24,256]{3,2,1,0:T(8,128)(2,1)} %get-tuple-element.29) | copy-start | bytes 589828
  129.9 1.9 %copy-start.5 = (bf16[2,8,24,256]{3,2,1,0:T(8,128)(2,1)S(1)}, bf16[2,8,24,256]{3,2,1,0:T(8,128)(2,1)}, u32[]{:S(2)}) copy-start(bf16[2,8,24,256]{3,2,1,0:T(8,128)(2,1)} %get-tuple-element.32) | copy-start | bytes 589828
  130.1 1.9 %copy-start.4 = (bf16[2,8,24,256]{3,2,1,0:T(8,128)(2,1)S(1)}, bf16[2,8,24,256]{3,2,1,0:T(8,128)(2,1)}, u32[]{:S(2)}) copy-start(bf16[2,8,24,256]{3,2,1,0:T(8,128)(2,1)} %get-tuple-element.30) | copy-start | bytes 589828
  130.4 1.9 %copy-start.3 = (bf16[2,8,24,256]{3,2,1,0:T(8,128)(2,1)S(1)}, bf16[2,8,24,256]{3,2,1,0:T(8,128)(2,1)}, u32[]{:S(2)}) copy-start(bf16[2,8,24,256]{3,2,1,0:T(8,128)(2,1)} %get-tuple-element.31) | copy-start | bytes 589828
  130.7 1.9 %copy-start.2 = (bf16[2,8,24,256]{3,2,1,0:T(8,128)(2,1)S(1)}, bf16[2,8,24,256]{3,2,1,0:T(8,128)(2,1)}, u32[]{:S(2)}) copy-start(bf16[2,8,24,256]{3,2,1,0:T(8,128)(2,1)} %get-tuple-element.28) | copy-start | bytes 589828
  131.2 2.8 %copy-start.9 = (s32[4]{0:T(128)S(1)}, s32[4]{0:T(128)}, u32[]{:S(2)}) copy-start(s32[4]{0:T(128)} %param.11) | copy-start | bytes 52
  131.2 9.4 %copy-start.12 = (f32[256]{0:T(256)S(1)}, f32[256]{0:T(256)}, u32[]{:S(2)}) copy-start(f32[256]{0:T(256)} %param.10) | copy-start | bytes 3076
  141.7 5.2 %collective-permute-start.3 = (bf16[2,8,4,256]{3,2,1,0:T(4,128)(2,1)S(1)}, bf16[2,8,4,256]{3,2,1,0:T(4,128)(2,1)S(1)}, u32[]{:S(2)}, u32[]{:S(2)}) collective-permute-start(bf16[2,8,4,256]{3,2,1,0:T(4,128)(2,1)S(1)} %get-tuple-element.38), channel_id=1, source_target_pairs={{0,4},{4,8},{8,12},{1,5},{5,9},{9,13},{2,6},{6,10},{10,14},{3,7},{... | collective-permute-start | bytes 98312 | tf_op jit(solution)/shard_map/ppermute | solution.py:17
  145.4 5.8 %collective-permute-start.4 = (bf16[2,8,4,256]{3,2,1,0:T(4,128)(2,1)S(1)}, bf16[2,8,4,256]{3,2,1,0:T(4,128)(2,1)S(1)}, u32[]{:S(2)}, u32[]{:S(2)}) collective-permute-start(bf16[2,8,4,256]{3,2,1,0:T(4,128)(2,1)S(1)} %get-tuple-element.39), channel_id=1, source_target_pairs={{4,0},{8,4},{12,8},{5,1},{9,5},{13,9},{6,2},{10,6},{14,10},{7,3},{... | collective-permute-start | bytes 98312 | tf_op jit(solution)/shard_map/ppermute | solution.py:18
Sparse Core Ops, SparseCore 0:
  9.5 111.4 all-gather.1
  134.2 6.4 reduce-scatter.1
where the time goes:
time: 159 us
  waiting for transfers between devices  101 us (64%)
  between operations  15.8 us (10%)
  starting transfers between devices  14.6 us (9%)
  matrix products  12.6 us (8%)
  other arithmetic  7.56 us (5%)
  local copies, waits for them, and re-layouts  7.04 us (4%)
    all_gather x1, waiting for transfers between devices, on_device(): lax.all_gather(kernel, ('tile', 'tm'), axis=3, tiled=True)  81.3 us
    dot_general x27, matrix products, conv_taps(): jnp.dot(window.reshape(-1, in_width), kernel_part[tap_time, tap_row, tap_...  12.6 us
    ppermute x2, starting transfers between devices, with_halo(): before = lax.ppermute(last, axis, up)  8.55 us
    ppermute x2, waiting for transfers between devices, with_halo(): after = lax.ppermute(leading, axis, down)  8.46 us
    ppermute x1, waiting for transfers between devices, passed_along(): return lax.ppermute(block, axis, route)  5.61 us
    reduce_scatter x1, waiting for transfers between devices, on_device(): summed = lax.psum_scatter(joined, 'ch', scatter_dimension=3, tiled=True)  4.61 us
    ppermute x1, starting transfers between devices, passed_along(): return lax.ppermute(block, axis, route)  3.41 us
  transfers between devices with their start and end apart: 7, of which 7 were waited for; matrix products, arithmetic and copies ran while one was open for 8% of the time, Pallas kernels for 0%

commit v1 on v0

--- a/solution.py
+++ b/solution.py
@@ -5,6 +5,27 @@
 
 GROUPS = 32
 RIM = 4
+
+
+def ring_gather(shard, axis, dim):
+    size, index, rows = (lax.axis_size(axis), lax.axis_index(axis), shard.shape[dim])
+    ahead = [(i, (i + 1) % size) for i in range(size)]
+    backward = [(i, (i - 1) % size) for i in range(size)]
+    filled = jnp.zeros((*shard.shape[:dim], size * rows, *shard.shape[dim + 1 :]), shard.dtype)
+    filled = lax.dynamic_update_slice_in_dim(filled, shard, index * rows, axis=dim)
+    from_left = from_right = shard
+    halfway = size // 2
+    for step in range(1, halfway + 1):
+        from_left = lax.ppermute(from_left, axis, ahead)
+        filled = lax.dynamic_update_slice_in_dim(
+            filled, from_left, (index - step) % size * rows, axis=dim
+        )
+        if step < size - halfway:
+            from_right = lax.ppermute(from_right, axis, backward)
+            filled = lax.dynamic_update_slice_in_dim(
+                filled, from_right, (index + step) % size * rows, axis=dim
+            )
+    return filled
 
 
 def with_halo(shard, sides, width):
@@ -103,7 +124,7 @@
             )
         )
 
-    totals = accumulate(lax.all_gather(kernel, ("tile", "tm"), axis=3, tiled=True))
+    totals = accumulate(ring_gather(kernel, ("tile", "tm"), 3))
     shaped = [
         running.reshape(frame_count, row_count, width_cols, out_chans)
         for running, width_cols in zip(totals, widths)

time: 159 us -> 219 us (1.38)
  matrix products: 12.6 us -> 34.1 us
  local copies, waits for them, and re-layouts: 7.04 us -> 23 us
  starting transfers between devices: 14.6 us -> 29.6 us
  waiting for transfers between devices: 101 us -> 107 us
    ppermute x0 -> x7, waiting for transfers between devices: none -> 85.8 us  [the longest x4 54.8 us: ring_gather(): from_left = lax.ppermute(from_left, axis, ahead)]
    all_gather x1 -> x0, waiting for transfers between devices: 81.3 us -> none  [on_device(): lax.all_gather(kernel, ('tile', 'tm'), axis=3, tiled=True)]
    dot_general x27, matrix products: 12.6 us -> 34.1 us  [conv_taps(): jnp.dot(window.reshape(-1, in_width), kernel_part[tap_time, tap_row, tap_...]
    ppermute x0 -> x7, starting transfers between devices: none -> 19 us  [the longest x3 11.1 us: ring_gather(): from_right = lax.ppermute(from_right, axis, backward)]
    dynamic_update_slice x0 -> x8, local copies, waits for them, and re-layouts: none -> 14.3 us  [the longest x4 7.72 us: ring_gather(): lax.dynamic_update_slice_in_dim(filled, from_left, (index - step) % size...]
    ppermute x1, waiting for transfers between devices: 5.61 us -> 13.1 us  [passed_along(): return lax.ppermute(block, axis, route)]
    ppermute x2, waiting for transfers between devices: 8.46 us -> 4.23 us  [with_halo(): after = lax.ppermute(leading, axis, down)]
    broadcast_in_dim x0 -> x1, local copies, waits for them, and re-layouts: none -> 3.68 us  [ring_gather(): jnp.zeros((*shard.shape[:dim], size * rows, *shard.shape[dim + 1:]), shar...]
  transfers between devices with their start and end apart: 7 -> 13, of which waited for: 7 -> 8; matrix products, arithmetic and copies ran while one was open for 8% -> 13% of each run, Pallas kernels for 0% -> 0%
where the time goes in v1:
time: 219 us; the launch traced here: 217 us
  waiting for transfers between devices  107 us (49%)
  matrix products  34.1 us (16%)
  starting transfers between devices  29.6 us (14%)
  local copies, waits for them, and re-layouts  23 us (11%)
  between operations  15.9 us (7%)
  other arithmetic  7.55 us (3%)
    ppermute x4, waiting for transfers between devices, ring_gather(): from_left = lax.ppermute(from_left, axis, ahead)  54.8 us
    dot_general x27, matrix products, conv_taps(): jnp.dot(window.reshape(-1, in_width), kernel_part[tap_time, tap_row, tap_...  34.1 us
    ppermute x3, waiting for transfers between devices, ring_gather(): from_right = lax.ppermute(from_right, axis, backward)  31 us
    ppermute x1, waiting for transfers between devices, passed_along(): return lax.ppermute(block, axis, route)  13.1 us
    ppermute x3, starting transfers between devices, ring_gather(): from_right = lax.ppermute(from_right, axis, backward)  11.1 us
    ppermute x4, starting transfers between devices, ring_gather(): from_left = lax.ppermute(from_left, axis, ahead)  7.9 us
    dynamic_update_slice x4, local copies, waits for them, and re-layouts, ring_gather(): lax.dynamic_update_slice_in_dim(filled, from_left, (index - step) % size...  7.72 us
    ppermute x2, starting transfers between devices, with_halo(): before = lax.ppermute(last, axis, up)  5.48 us
  transfers between devices with their start and end apart: 13, of which 8 were waited for; matrix products, arithmetic and copies ran while one was open for 13% of the time, Pallas kernels for 0%

profile of v1, /device:TPU:0, one launch (start us, length us, event | category | flops | bytes accessed | tf_op | source)
XLA Modules:
  0.0 217.3 jit_solution(3927187382463621431)
XLA Ops:
  6.5 2.9 %collective-permute-start.3 = (bf16[3,3,3,32,512]{4,3,2,1,0:T(8,128)(2,1)}, bf16[3,3,3,32,512]{4,3,2,1,0:T(8,128)(2,1)}, u32[]{:S(2)}, u32[]{:S(2)}) collective-permute-start(bf16[3,3,3,32,512]{4,3,2,1,0:T(8,128)(2,1)} %param.9), channel_id=1, source_target_pairs={{0,2},{2,4},{4,6},{6,8},{8,10},{10,12},{12,14},{14,0},{1,3},{3,5},... | collective-permute-start | bytes 2654216 | tf_op jit(solution)/shard_map/ppermute | solution.py:19
  9.5 3.0 %collective-permute-start.4 = (bf16[3,3,3,32,512]{4,3,2,1,0:T(8,128)(2,1)}, bf16[3,3,3,32,512]{4,3,2,1,0:T(8,128)(2,1)}, u32[]{:S(2)}, u32[]{:S(2)}) collective-permute-start(bf16[3,3,3,32,512]{4,3,2,1,0:T(8,128)(2,1)} %param.9), channel_id=1, source_target_pairs={{0,14},{2,0},{4,2},{6,4},{8,6},{10,8},{12,10},{14,12},{1,15},{3,1}... | collective-permute-start | bytes 2654216 | tf_op jit(solution)/shard_map/ppermute | solution.py:24
  12.5 0.9 fusion.62
  13.4 1.9 collective-permute-start
  15.3 1.3 collective-permute-start.1
  18.5 29.1 %collective-permute-done.3 = bf16[3,3,3,32,512]{4,3,2,1,0:T(8,128)(2,1)} collective-permute-done((bf16[3,3,3,32,512]{4,3,2,1,0:T(8,128)(2,1)}, bf16[3,3,3,32,512]{4,3,2,1,0:T(8,128)(2,1)}, u32[]{:S(2)}, u32[]{:S(2)}) %collective-permute-start.3) | collective-permute-done | bytes 884768 | tf_op jit(solution)/shard_map/ppermute | solution.py:19
  47.7 2.5 %collective-permute-start.5 = (bf16[3,3,3,32,512]{4,3,2,1,0:T(8,128)(2,1)}, bf16[3,3,3,32,512]{4,3,2,1,0:T(8,128)(2,1)}, u32[]{:S(2)}, u32[]{:S(2)}) collective-permute-start(bf16[3,3,3,32,512]{4,3,2,1,0:T(8,128)(2,1)} %collective-permute-done.3), channel_id=1, source_target_pairs={{0,2},{2,4},{4,6},{6,8},{8,10},{10,12},{12,14},{14,0},{1,3},{3,5},... | collective-permute-start | bytes 2654216 | tf_op jit(solution)/shard_map/ppermute | solution.py:19
  50.1 1.0 pad_maximum_fusion.1
  51.1 2.5 %collective-permute-start.2 = (bf16[2,8,24,256]{3,2,1,0:T(8,128)(2,1)S(1)}, bf16[2,8,24,256]{3,2,1,0:T(8,128)(2,1)S(1)}, u32[]{:S(2)}, u32[]{:S(2)}) collective-permute-start(bf16[2,8,24,256]{3,2,1,0:T(8,128)(2,1)S(1)} %pad_maximum_fusion.1), channel_id=1, source_target_pairs={{0,2},{1,3},{4,6},{5,7},{8,10},{9,11},{12,14},{13,15},{16,18},{17,... | collective-permute-start | bytes 589832 | tf_op jit(solution)/shard_map/ppermute | solution.py:47
  53.6 3.7 %broadcast_in_dim.6 = bf16[3,3,3,256,512]{4,3,2,1,0:T(8,128)(2,1)} broadcast(bf16[]{:T(256)} %constant.92.clone.1), dimensions={} | broadcast | bytes 7077890 | tf_op jit(solution)/shard_map/broadcast_in_dim | solution.py:14
  57.3 1.1 constant_dynamic-update-slice_fusion.7
  58.4 1.1 concatenate.24
  59.5 13.1 %collective-permute-done.2 = bf16[2,8,24,256]{3,2,1,0:T(8,128)(2,1)S(1)} collective-permute-done((bf16[2,8,24,256]{3,2,1,0:T(8,128)(2,1)S(1)}, bf16[2,8,24,256]{3,2,1,0:T(8,128)(2,1)S(1)}, u32[]{:S(2)}, u32[]{:S(2)}) %collective-permute-start.2) | collective-permute-done | bytes 196640 | tf_op jit(solution)/shard_map/ppermute | solution.py:47
  72.6 1.1 concatenate.23
  73.7 1.2 fusion
  74.9 5.5 %collective-permute-start.6 = (bf16[3,3,3,32,512]{4,3,2,1,0:T(8,128)(2,1)}, bf16[3,3,3,32,512]{4,3,2,1,0:T(8,128)(2,1)}, u32[]{:S(2)}, u32[]{:S(2)}) collective-permute-start(bf16[3,3,3,32,512]{4,3,2,1,0:T(8,128)(2,1)} %collective-permute-done.4), channel_id=1, source_target_pairs={{0,14},{2,0},{4,2},{6,4},{8,6},{10,8},{12,10},{14,12},{1,15},{3,1}... | collective-permute-start | bytes 2654216 | tf_op jit(solution)/shard_map/ppermute | solution.py:24
  80.4 1.7 fusion.3
  82.5 1.1 multiply_convert_fusion
  83.6 30.9 %collective-permute-done.6 = bf16[3,3,3,32,512]{4,3,2,1,0:T(8,128)(2,1)} collective-permute-done((bf16[3,3,3,32,512]{4,3,2,1,0:T(8,128)(2,1)}, bf16[3,3,3,32,512]{4,3,2,1,0:T(8,128)(2,1)}, u32[]{:S(2)}, u32[]{:S(2)}) %collective-permute-start.6) | collective-permute-done | bytes 884768 | tf_op jit(solution)/shard_map/ppermute | solution.py:24
  114.5 2.6 %collective-permute-start.8 = (bf16[3,3,3,32,512]{4,3,2,1,0:T(8,128)(2,1)}, bf16[3,3,3,32,512]{4,3,2,1,0:T(8,128)(2,1)S(1)}, u32[]{:S(2)}, u32[]{:S(2)}) collective-permute-start(bf16[3,3,3,32,512]{4,3,2,1,0:T(8,128)(2,1)} %collective-permute-done.6), channel_id=1, source_target_pairs={{0,14},{2,0},{4,2},{6,4},{8,6},{10,8},{12,10},{14,12},{1,15},{3,1}... | collective-permute-start | bytes 2654216 | tf_op jit(solution)/shard_map/ppermute | solution.py:24
  117.2 16.4 %collective-permute-done.7 = bf16[3,3,3,32,512]{4,3,2,1,0:T(8,128)(2,1)} collective-permute-done((bf16[3,3,3,32,512]{4,3,2,1,0:T(8,128)(2,1)}, bf16[3,3,3,32,512]{4,3,2,1,0:T(8,128)(2,1)}, u32[]{:S(2)}, u32[]{:S(2)}) %collective-permute-start.7) | collective-permute-done | bytes 884768 | tf_op jit(solution)/shard_map/ppermute | solution.py:19
  133.6 2.5 %collective-permute-start.9 = (bf16[3,3,3,32,512]{4,3,2,1,0:T(8,128)(2,1)}, bf16[3,3,3,32,512]{4,3,2,1,0:T(8,128)(2,1)S(1)}, u32[]{:S(2)}, u32[]{:S(2)}) collective-permute-start(bf16[3,3,3,32,512]{4,3,2,1,0:T(8,128)(2,1)} %collective-permute-done.7), channel_id=1, source_target_pairs={{0,2},{2,4},{4,6},{6,8},{8,10},{10,12},{12,14},{14,0},{1,3},{3,5},... | collective-permute-start | bytes 2654216 | tf_op jit(solution)/shard_map/ppermute | solution.py:19
  136.5 2.3 %constant_dynamic-update-slice_fusion.6 = bf16[3,3,3,256,512]{4,3,2,1,0:T(8,128)(2,1)} fusion(bf16[3,3,3,256,512]{4,3,2,1,0:T(8,128)(2,1)} %constant_dynamic-update-slice_fusion.7, bf16[3,3,3,32,512]{4,3,2,1,0:T(8,128)(2,1)} %collective-permute-done.3, s32[]{:T(128)S(6)} %select_n.90), kind=kLoop, calls=%fused_computation.128 | loop fusion | bytes 1769476 | tf_op jit(solution)/shard_map/dynamic_update_slice | solution.py:20
  138.8 2.2 %constant_dynamic-update-slice_fusion.5 = bf16[3,3,3,256,512]{4,3,2,1,0:T(8,128)(2,1)} fusion(bf16[3,3,3,256,512]{4,3,2,1,0:T(8,128)(2,1)} %constant_dynamic-update-slice_fusion.6, bf16[3,3,3,32,512]{4,3,2,1,0:T(8,128)(2,1)} %collective-permute-done.4, s32[]{:T(128)S(6)} %select_n.92), kind=kLoop, calls=%fused_computation.127 | loop fusion | bytes 1769476 | tf_op jit(solution)/shard_map/dynamic_update_slice | solution.py:25
  141.0 2.2 %constant_dynamic-update-slice_fusion.4 = bf16[3,3,3,256,512]{4,3,2,1,0:T(8,128)(2,1)} fusion(bf16[3,3,3,256,512]{4,3,2,1,0:T(8,128)(2,1)} %constant_dynamic-update-slice_fusion.5, bf16[3,3,3,32,512]{4,3,2,1,0:T(8,128)(2,1)} %collective-permute-done.5, s32[]{:T(128)S(6)} %select_n.94), kind=kLoop, calls=%fused_computation.126 | loop fusion | bytes 1769476 | tf_op jit(solution)/shard_map/dynamic_update_slice | solution.py:20
  143.3 2.2 %constant_dynamic-update-slice_fusion.3 = bf16[3,3,3,256,512]{4,3,2,1,0:T(8,128)(2,1)} fusion(bf16[3,3,3,256,512]{4,3,2,1,0:T(8,128)(2,1)} %constant_dynamic-update-slice_fusion.4, bf16[3,3,3,32,512]{4,3,2,1,0:T(8,128)(2,1)} %collective-permute-done.6, s32[]{:T(128)S(6)} %select_n.96), kind=kLoop, calls=%fused_computation.125 | loop fusion | bytes 1769476 | tf_op jit(solution)/shard_map/dynamic_update_slice | solution.py:25
  145.5 2.2 %constant_dynamic-update-slice_fusion.2 = bf16[3,3,3,256,512]{4,3,2,1,0:T(8,128)(2,1)} fusion(bf16[3,3,3,256,512]{4,3,2,1,0:T(8,128)(2,1)} %constant_dynamic-update-slice_fusion.3, bf16[3,3,3,32,512]{4,3,2,1,0:T(8,128)(2,1)} %collective-permute-done.7, s32[]{:T(128)S(6)} %select_n.98), kind=kLoop, calls=%fused_computation.124 | loop fusion | bytes 1769476 | tf_op jit(solution)/shard_map/dynamic_update_slice | solution.py:20
  147.7 1.0 constant_dynamic-update-slice_fusion.1
  148.7 9.3 %collective-permute-done.9 = bf16[3,3,3,32,512]{4,3,2,1,0:T(8,128)(2,1)S(1)} collective-permute-done((bf16[3,3,3,32,512]{4,3,2,1,0:T(8,128)(2,1)}, bf16[3,3,3,32,512]{4,3,2,1,0:T(8,128)(2,1)S(1)}, u32[]{:S(2)}, u32[]{:S(2)}) %collective-permute-start.9) | collective-permute-done | bytes 884768 | tf_op jit(solution)/shard_map/ppermute | solution.py:19
  158.0 1.0 constant_dynamic-update-slice_fusion
  159.0 1.2 fusion.35
  160.2 1.2 fusion.36
  161.4 1.2 fusion.37
  162.6 1.2 fusion.38
  163.8 1.2 fusion.39
  165.1 1.2 fusion.40
  166.3 1.2 fusion.41
  167.5 1.2 fusion.43
  168.7 1.2 fusion.44
  169.9 1.2 fusion.45
  171.1 1.2 fusion.46
  172.3 1.2 fusion.47
  173.5 1.2 fusion.48
  174.7 1.2 fusion.49
  175.9 1.2 fusion.50
  177.1 1.2 fusion.52
  178.3 1.2 fusion.53
  179.6 1.2 fusion.54
  180.8 1.2 fusion.42
  182.0 1.2 fusion.51
  183.2 1.2 fusion.34
  184.4 1.2 fusion.33
  185.6 1.2 fusion.32
  186.8 1.2 fusion.31
  188.0 1.2 fusion.30
  189.2 1.2 fusion.29
  190.5 2.9 %fusion.28 = f32[384,512]{1,0:T(8,128)} fusion(f32[384,512]{1,0:T(8,128)S(1)} %fusion.29, f32[384,512]{1,0:T(8,128)S(1)} %fusion.30, f32[384,512]{1,0:T(8,128)S(1)} %fusion.31, f32[384,512]{1,0:T(8,128)S(1)} %fusion.32, f32[384,512]{1,0:T(8,128)S(1)} %fusion.33, f32[384,512]{1,0:T(8,128)S(1)} %fusion.34, f32[384,512]{1,0:T(8,128)S(1)} %fusion.35, ...), kind=kOutput, calls=%fused_computation.56 | convolution fusion | flops 105775104 | bytes 21692416 | tf_op jit(solution)/shard_map/dot_general | solution.py:89
  193.4 0.6 fusion.63
  195.4 3.7 %reduce-scatter.2.cloned.1.call-done = f32[2,8,24,256]{3,2,1,0:T(8,128)} async-done(((f32[2,8,24,512]{3,2,1,0:T(8,128)}), f32[2,8,24,256]{3,2,1,0:T(8,128)}) %reduce-scatter.2.cloned.1.call-update) | async-done | bytes 393232 | tf_op jit(solution)/shard_map/reduce_scatter | solution.py:133
  199.1 1.0 add_convert_fusion
  200.2 3.6 %collective-permute-start.10 = (bf16[2,8,4,256]{3,2,1,0:T(4,128)(2,1)S(1)}, bf16[2,8,4,256]{3,2,1,0:T(4,128)(2,1)S(1)}, u32[]{:S(2)}, u32[]{:S(2)}) collective-permute-start(bf16[2,8,4,256]{3,2,1,0:T(4,128)(2,1)S(1)} %get-tuple-element.38), channel_id=1, source_target_pairs={{0,4},{4,8},{8,12},{1,5},{5,9},{9,13},{2,6},{6,10},{10,14},{3,7},{... | collective-permute-start | bytes 98312 | tf_op jit(solution)/shard_map/ppermute | solution.py:38
  203.8 1.3 collective-permute-start.11
  205.3 4.2 %collective-permute-done.11 = bf16[2,8,4,256]{3,2,1,0:T(4,128)(2,1)S(1)} collective-permute-done((bf16[2,8,4,256]{3,2,1,0:T(4,128)(2,1)S(1)}, bf16[2,8,4,256]{3,2,1,0:T(4,128)(2,1)S(1)}, u32[]{:S(2)}, u32[]{:S(2)}) %collective-permute-start.11) | collective-permute-done | bytes 32800 | tf_op jit(solution)/shard_map/ppermute | solution.py:39
  209.7 0.7 pad_maximum_fusion.2
  (38 shorter events, 2.5 us)
Async XLA Ops:
  6.5 50.8 %copy-start = (bf16[3,3,3,32,512]{4,3,2,1,0:T(8,128)(2,1)S(1)}, bf16[3,3,3,32,512]{4,3,2,1,0:T(8,128)(2,1)}, u32[]{:S(2)}) copy-start(bf16[3,3,3,32,512]{4,3,2,1,0:T(8,128)(2,1)} %param.9) | copy-start | bytes 2654212
  6.5 192.5 %reduce-scatter.2.cloned.1.call-start = ((), (), s32[]{:S(2)}) async-start(), calls=%async_computation.1 | async-start | bytes 1179648 | tf_op jit(solution)/shard_map/reduce_scatter | solution.py:133
  6.5 41.1 %collective-permute-start.3 = (bf16[3,3,3,32,512]{4,3,2,1,0:T(8,128)(2,1)}, bf16[3,3,3,32,512]{4,3,2,1,0:T(8,128)(2,1)}, u32[]{:S(2)}, u32[]{:S(2)}) collective-permute-start(bf16[3,3,3,32,512]{4,3,2,1,0:T(8,128)(2,1)} %param.9), channel_id=1, source_target_pairs={{0,2},{2,4},{4,6},{6,8},{8,10},{10,12},{12,14},{14,0},{1,3},{3,5},... | collective-permute-start | bytes 2654216 | tf_op jit(solution)/shard_map/ppermute | solution.py:19
  9.5 65.4 %collective-permute-start.4 = (bf16[3,3,3,32,512]{4,3,2,1,0:T(8,128)(2,1)}, bf16[3,3,3,32,512]{4,3,2,1,0:T(8,128)(2,1)}, u32[]{:S(2)}, u32[]{:S(2)}) collective-permute-start(bf16[3,3,3,32,512]{4,3,2,1,0:T(8,128)(2,1)} %param.9), channel_id=1, source_target_pairs={{0,14},{2,0},{4,2},{6,4},{8,6},{10,8},{12,10},{14,12},{1,15},{3,1}... | collective-permute-start | bytes 2654216 | tf_op jit(solution)/shard_map/ppermute | solution.py:24
  13.4 36.7 %collective-permute-start = (bf16[2,8,4,256]{3,2,1,0:T(4,128)(2,1)S(1)}, bf16[2,8,4,256]{3,2,1,0:T(4,128)(2,1)S(1)}, u32[]{:S(2)}, u32[]{:S(2)}) collective-permute-start(bf16[2,8,4,256]{3,2,1,0:T(4,128)(2,1)S(1)} %get-tuple-element.40), channel_id=1, source_target_pairs={{0,4},{4,8},{8,12},{1,5},{5,9},{9,13},{2,6},{6,10},{10,14},{3,7},{... | collective-permute-start | bytes 98312 | tf_op jit(solution)/shard_map/ppermute | solution.py:38
  15.3 34.8 %collective-permute-start.1 = (bf16[2,8,4,256]{3,2,1,0:T(4,128)(2,1)S(1)}, bf16[2,8,4,256]{3,2,1,0:T(4,128)(2,1)S(1)}, u32[]{:S(2)}, u32[]{:S(2)}) collective-permute-start(bf16[2,8,4,256]{3,2,1,0:T(4,128)(2,1)S(1)} %get-tuple-element.41), channel_id=1, source_target_pairs={{4,0},{8,4},{12,8},{5,1},{9,5},{13,9},{6,2},{10,6},{14,10},{7,3},{... | collective-permute-start | bytes 98312 | tf_op jit(solution)/shard_map/ppermute | solution.py:39
  47.7 32.7 %collective-permute-start.5 = (bf16[3,3,3,32,512]{4,3,2,1,0:T(8,128)(2,1)}, bf16[3,3,3,32,512]{4,3,2,1,0:T(8,128)(2,1)}, u32[]{:S(2)}, u32[]{:S(2)}) collective-permute-start(bf16[3,3,3,32,512]{4,3,2,1,0:T(8,128)(2,1)} %collective-permute-done.3), channel_id=1, source_target_pairs={{0,2},{2,4},{4,6},{6,8},{8,10},{10,12},{12,14},{14,0},{1,3},{3,5},... | collective-permute-start | bytes 2654216 | tf_op jit(solution)/shard_map/ppermute | solution.py:19
  51.1 21.5 %collective-permute-start.2 = (bf16[2,8,24,256]{3,2,1,0:T(8,128)(2,1)S(1)}, bf16[2,8,24,256]{3,2,1,0:T(8,128)(2,1)S(1)}, u32[]{:S(2)}, u32[]{:S(2)}) collective-permute-start(bf16[2,8,24,256]{3,2,1,0:T(8,128)(2,1)S(1)} %pad_maximum_fusion.1), channel_id=1, source_target_pairs={{0,2},{1,3},{4,6},{5,7},{8,10},{9,11},{12,14},{13,15},{16,18},{17,... | collective-permute-start | bytes 589832 | tf_op jit(solution)/shard_map/ppermute | solution.py:47
  57.3 25.2 %copy-start.1 = (bf16[2,8,16,256]{3,2,1,0:T(8,128)(2,1)S(1)}, bf16[2,8,16,256]{3,2,1,0:T(8,128)(2,1)}, u32[]{:S(2)}) copy-start(bf16[2,8,16,256]{3,2,1,0:T(8,128)(2,1)} %param.6) | copy-start | bytes 393220
  57.3 25.2 %copy-start.3 = (f32[256]{0:T(256)S(1)}, f32[256]{0:T(256)}, u32[]{:S(2)}) copy-start(f32[256]{0:T(256)} %param.8) | copy-start | bytes 3076
  57.3 25.2 %copy-start.4 = (f32[256]{0:T(256)S(1)}, f32[256]{0:T(256)}, u32[]{:S(2)}) copy-start(f32[256]{0:T(256)} %param.7) | copy-start | bytes 3076
  74.9 39.6 %collective-permute-start.6 = (bf16[3,3,3,32,512]{4,3,2,1,0:T(8,128)(2,1)}, bf16[3,3,3,32,512]{4,3,2,1,0:T(8,128)(2,1)}, u32[]{:S(2)}, u32[]{:S(2)}) collective-permute-start(bf16[3,3,3,32,512]{4,3,2,1,0:T(8,128)(2,1)} %collective-permute-done.4), channel_id=1, source_target_pairs={{0,14},{2,0},{4,2},{6,4},{8,6},{10,8},{12,10},{14,12},{1,15},{3,1}... | collective-permute-start | bytes 2654216 | tf_op jit(solution)/shard_map/ppermute | solution.py:24
  80.4 53.2 %collective-permute-start.7 = (bf16[3,3,3,32,512]{4,3,2,1,0:T(8,128)(2,1)}, bf16[3,3,3,32,512]{4,3,2,1,0:T(8,128)(2,1)}, u32[]{:S(2)}, u32[]{:S(2)}) collective-permute-start(bf16[3,3,3,32,512]{4,3,2,1,0:T(8,128)(2,1)} %collective-permute-done.5), channel_id=1, source_target_pairs={{0,2},{2,4},{4,6},{6,8},{8,10},{10,12},{12,14},{14,0},{1,3},{3,5},... | collective-permute-start | bytes 2654216 | tf_op jit(solution)/shard_map/ppermute | solution.py:19
  114.5 33.1 %collective-permute-start.8 = (bf16[3,3,3,32,512]{4,3,2,1,0:T(8,128)(2,1)}, bf16[3,3,3,32,512]{4,3,2,1,0:T(8,128)(2,1)S(1)}, u32[]{:S(2)}, u32[]{:S(2)}) collective-permute-start(bf16[3,3,3,32,512]{4,3,2,1,0:T(8,128)(2,1)} %collective-permute-done.6), channel_id=1, source_target_pairs={{0,14},{2,0},{4,2},{6,4},{8,6},{10,8},{12,10},{14,12},{1,15},{3,1}... | collective-permute-start | bytes 2654216 | tf_op jit(solution)/shard_map/ppermute | solution.py:24
  133.6 24.3 %collective-permute-start.9 = (bf16[3,3,3,32,512]{4,3,2,1,0:T(8,128)(2,1)}, bf16[3,3,3,32,512]{4,3,2,1,0:T(8,128)(2,1)S(1)}, u32[]{:S(2)}, u32[]{:S(2)}) collective-permute-start(bf16[3,3,3,32,512]{4,3,2,1,0:T(8,128)(2,1)} %collective-permute-done.7), channel_id=1, source_target_pairs={{0,2},{2,4},{4,6},{6,8},{8,10},{10,12},{12,14},{14,0},{1,3},{3,5},... | collective-permute-start | bytes 2654216 | tf_op jit(solution)/shard_map/ppermute | solution.py:19
  190.4 3.0 %copy-start.2 = (s32[4]{0:T(128)S(1)}, s32[4]{0:T(128)}, u32[]{:S(2)}) copy-start(s32[4]{0:T(128)} %param.11) | copy-start | bytes 52
  190.4 8.6 %copy-start.5 = (f32[256]{0:T(256)S(1)}, f32[256]{0:T(256)}, u32[]{:S(2)}) copy-start(f32[256]{0:T(256)} %param.10) | copy-start | bytes 3076
  200.2 5.2 %collective-permute-start.10 = (bf16[2,8,4,256]{3,2,1,0:T(4,128)(2,1)S(1)}, bf16[2,8,4,256]{3,2,1,0:T(4,128)(2,1)S(1)}, u32[]{:S(2)}, u32[]{:S(2)}) collective-permute-start(bf16[2,8,4,256]{3,2,1,0:T(4,128)(2,1)S(1)} %get-tuple-element.38), channel_id=1, source_target_pairs={{0,4},{4,8},{8,12},{1,5},{5,9},{9,13},{2,6},{6,10},{10,14},{3,7},{... | collective-permute-start | bytes 98312 | tf_op jit(solution)/shard_map/ppermute | solution.py:38
  203.8 5.8 %collective-permute-start.11 = (bf16[2,8,4,256]{3,2,1,0:T(4,128)(2,1)S(1)}, bf16[2,8,4,256]{3,2,1,0:T(4,128)(2,1)S(1)}, u32[]{:S(2)}, u32[]{:S(2)}) collective-permute-start(bf16[2,8,4,256]{3,2,1,0:T(4,128)(2,1)S(1)} %get-tuple-element.39), channel_id=1, source_target_pairs={{4,0},{8,4},{12,8},{5,1},{9,5},{13,9},{6,2},{10,6},{14,10},{7,3},{... | collective-permute-start | bytes 98312 | tf_op jit(solution)/shard_map/ppermute | solution.py:39
Sparse Core Ops, SparseCore 0:
  193.5 5.5 reduce-scatter.1
